TPU v7x, 32 devices: a whole 2x2x4 slice. The times are simulated.
32 devices in a mesh: section: 4 (over y, x), seq: 8 (over z, core).
Axes of the slice: x: 2, y: 2, z: 4, core: 2. Of those that a mesh axis runs over, the one named last changes fastest.
Arguments:
- inputs: bfloat16 [4, 4096, 1536], P(None, 'seq'), may hold values from -40 to 40
- weights: bfloat16 [2, 5, 1536, 1536], P(None, None, None, 'section'), may hold values from -0.0625 to 0.0625
- gains: float32 [2, 1536], replicated, may hold values from 0.1 to 1.9
Outputs:
- activations: bfloat16 [2, 4, 4096, 1536], P(None, None, 'seq', 'section')
All inputs are finite; a program needn't handle non-finite values.
Results may differ from a plain program's by a relative error of at most 0.0044.
Values may be sent and summed in bfloat16 or wider, within the bound.
A program may use at most 128 MiB of HBM per device.

v0:
```python
import jax
import jax.numpy as jnp
from jax import lax
from jax.sharding import PartitionSpec as P


def with_halo(value, sides, width):
    for axis, dim in sides:
        count, length = (lax.axis_size(axis), value.shape[dim])
        up = [(i, (i + 1) % count) for i in range(count - 1)]
        down = [(j, i) for i, j in up]
        last = lax.slice_in_dim(value, length - width, length, axis=dim)
        initial = lax.slice_in_dim(value, 0, width, axis=dim)
        before = lax.ppermute(last, axis, up)
        after = lax.ppermute(initial, axis, down)
        value = jnp.concatenate([before, value, after], axis=dim)
    return value


def convolve(padded, kernel):
    count = padded.shape[1] - 4
    total = jnp.zeros((padded.shape[0], count, kernel.shape[2]), jnp.float32)
    for k in range(5):
        total = total + jnp.einsum(
            "brc,co->bro", padded[:, k : k + count], kernel[k], preferred_element_type=jnp.float32
        )
    return total


def normed(current, gain):
    values = current.astype(jnp.float32)
    scale = lax.rsqrt(jnp.mean(values * values, axis=-1, keepdims=True) + 1e-06)
    return jax.nn.gelu(values * scale * gain).astype(jnp.bfloat16)


def neighbours(hidden):
    return with_halo(hidden, (("seq", 1),), 2)


def local(inputs, weights, gains):
    share = weights.shape[3]
    begin = lax.axis_index("section") * share
    hidden = normed(inputs, gains[0])
    conv = convolve(neighbours(hidden), weights[0])
    own = lax.dynamic_slice_in_dim(inputs, begin, share, 2)
    current = (own.astype(jnp.float32) + conv).astype(jnp.bfloat16)
    results = [current]
    kernel = weights[1]
    whole = lax.all_gather(current, "section", axis=2, tiled=True)
    conv = convolve(neighbours(normed(whole, gains[1])), kernel)
    current = (current.astype(jnp.float32) + conv).astype(jnp.bfloat16)
    results.append(current)
    return jnp.stack(results, axis=0)


def solution(mesh):
    in_specs = (P(None, "seq", None), P(None, None, None, "section"), P())
    out_specs = P(None, None, "seq", "section")
    return jax.shard_map(local, mesh=mesh, in_specs=in_specs, out_specs=out_specs, check_vma=False)
```

profile of v0, /device:TPU:16, one launch (start us, length us, event | category | flops | bytes accessed | tf_op | source)
XLA Modules:
  0.0 172.9 jit_solution(12097460315456413241)
XLA Ops:
  6.5 0.0 copy-start.4
  6.5 0.0 all-gather.2.cloned.1.call-start
  6.5 0.0 copy-start
  6.5 4.2 %fusion = f32[4,512]{1,0:T(4,128)S(1)} fusion(bf16[4,512,1536]{2,1,0:T(8,128)(2,1)} %param.3), kind=kLoop, calls=%fused_computation.6 | loop fusion | flops 9435136 | bytes 6299648 | tf_op jit(solution)/shard_map/reduce_sum | solution.py:32
  10.8 0.0 copy-done.4
  10.8 0.3 copy-done
  11.2 5.8 %fusion.4 = bf16[4,512,1536]{2,1,0:T(8,128)(2,1)S(1)} fusion(bf16[4,512,1536]{2,1,0:T(8,128)(2,1)S(1)} %copy-done, f32[1536]{0:T(1024)S(1)} %get-tuple-element.6, f32[4,512]{1,0:T(4,128)S(1)} %add_rsqrt_fusion.1), kind=kLoop, calls=%fused_computation.10 | loop fusion | flops 37748736 | bytes 12597248 | tf_op jit(solution)/shard_map/convert_element_type | solution.py:33
  16.9 0.0 copy-start.2
  17.0 1.9 %collective-permute-start = (bf16[4,2,1536]{2,1,0:T(2,128)(2,1)S(1)}, bf16[4,2,1536]{2,1,0:T(2,128)(2,1)S(1)}, u32[]{:S(2)}, u32[]{:S(2)}) collective-permute-start(bf16[4,2,1536]{2,1,0:T(2,128)(2,1)S(1)} %get-tuple-element.9), channel_id=1, source_target_pairs={{0,1},{1,2},{2,3},{3,4},{4,5},{5,6},{6,7},{8,9},{9,10},{10,11},{11... | collective-permute-start | bytes 73736 | tf_op jit(solution)/shard_map/ppermute | solution.py:14
  18.9 3.6 %collective-permute-start.1 = (bf16[4,2,1536]{2,1,0:T(2,128)(2,1)S(1)}, bf16[4,2,1536]{2,1,0:T(2,128)(2,1)S(1)}, u32[]{:S(2)}, u32[]{:S(2)}) collective-permute-start(bf16[4,2,1536]{2,1,0:T(2,128)(2,1)S(1)} %get-tuple-element.10), channel_id=1, source_target_pairs={{1,0},{2,1},{3,2},{4,3},{5,4},{6,5},{7,6},{9,8},{10,9},{11,10},{12... | collective-permute-start | bytes 73736 | tf_op jit(solution)/shard_map/ppermute | solution.py:15
  22.6 6.4 %fusion.53 = f32[4,512,384]{2,1,0:T(8,128)} fusion(bf16[4,512,1536]{2,1,0:T(8,128)(2,1)S(1)} %fusion.4, bf16[2,5,1536,384]{3,2,1,0:T(8,128)(2,1)} %param.4), kind=kOutput, calls=%fused_computation.66 | convolution fusion | flops 2415919104 | bytes 10616832 | tf_op jit(solution)/shard_map/brc,co->bro/dot_general | solution.py:24
  29.0 0.0 copy-done.2
  29.0 0.0 slice-start
  29.0 0.0 slice-start.1
  29.0 0.0 collective-permute-done
  29.0 6.2 %fusion.30 = f32[4,512,384]{2,1,0:T(8,128)S(1)} fusion(bf16[4,2,1536]{2,1,0:T(2,128)(2,1)S(1)} %collective-permute-done, bf16[4,512,1536]{2,1,0:T(8,128)(2,1)} %copy-done.2, bf16[2,5,1536,384]{3,2,1,0:T(8,128)(2,1)} %param.4), kind=kOutput, calls=%fused_computation.41 | convolution fusion | flops 2428502016 | bytes 10641408 | tf_op jit(solution)/shard_map/brc,co->bro/dot_general | solution.py:24
  35.1 0.0 slice-done
  35.2 0.0 slice-done.1
  35.2 4.8 %fusion.38 = f32[4,512,384]{2,1,0:T(8,128)S(1)} fusion(bf16[4,512,1536]{2,1,0:T(8,128)(2,1)S(1)} %bitcast.60, bf16[4,2,1536]{2,1,0:T(2,128)(2,1)S(1)} %collective-permute-done, bf16[2,5,1536,384]{3,2,1,0:T(8,128)(2,1)} %param.4), kind=kOutput, calls=%fused_computation.52 | convolution fusion | flops 2428502016 | bytes 10641408 | tf_op jit(solution)/shard_map/brc,co->bro/dot_general | solution.py:24
  40.0 0.0 copy-start.5
  40.0 0.0 collective-permute-done.1
  40.0 4.9 %fusion.27 = f32[4,512,384]{2,1,0:T(8,128)S(1)} fusion(bf16[4,512,1536]{2,1,0:T(8,128)(2,1)S(1)} %bitcast.60, bf16[4,2,1536]{2,1,0:T(2,128)(2,1)S(1)} %collective-permute-done.1, bf16[2,5,1536,384]{3,2,1,0:T(8,128)(2,1)} %param.4), kind=kOutput, calls=%fused_computation.39 | convolution fusion | flops 2428502016 | bytes 10641408 | tf_op jit(solution)/shard_map/brc,co->bro/dot_general | solution.py:24
  45.0 0.0 copy-done.5
  45.0 6.7 %add_convert_fusion.1 = bf16[4,512,384]{2,1,0:T(8,128)(2,1)} fusion(f32[4,512,384]{2,1,0:T(8,128)S(1)} %fusion.27, f32[4,512,384]{2,1,0:T(8,128)S(1)} %copy-done.5, f32[4,512,384]{2,1,0:T(8,128)S(1)} %fusion.30, f32[4,512,384]{2,1,0:T(8,128)S(1)} %fusion.38, bf16[4,512,1536]{2,1,0:T(8,128)(2,1)} %param.3, s32[]{:T(128)S(6)} %select_n.3, ...), kind=kOutput, calls=%fused_computation.56 | convolution fusion | flops 2434007040 | bytes 23224324 | tf_op jit(solution)/shard_map/brc,co->bro/dot_general | solution.py:24
  51.6 0.0 all-gather.2.cloned.1.call-update
  51.7 71.1 %all-gather.2.cloned.1.call-done = bf16[4,512,1536]{2,1,0:T(8,128)(2,1)} async-done(((bf16[4,512,384]{2,1,0:T(8,128)(2,1)}), bf16[4,512,1536]{2,1,0:T(8,128)(2,1)}) %all-gather.2.cloned.1.call-update) | async-done | bytes 6291472 | tf_op jit(solution)/shard_map/all_gather | solution.py:49
  122.8 0.0 copy-start.1
  122.8 4.2 %fusion.9 = f32[4,512]{1,0:T(4,128)S(1)} fusion(bf16[4,512,1536]{2,1,0:T(8,128)(2,1)} %all-gather.2.cloned.1.call-done), kind=kLoop, calls=%fused_computation.15 | loop fusion | flops 9435136 | bytes 6299648 | tf_op jit(solution)/shard_map/reduce_sum | solution.py:32
  127.0 0.4 copy-done.1
  127.4 5.8 %fusion.13 = bf16[4,512,1536]{2,1,0:T(8,128)(2,1)S(1)} fusion(bf16[4,512,1536]{2,1,0:T(8,128)(2,1)S(1)} %copy-done.1, f32[1536]{0:T(1024)S(1)} %get-tuple-element.5, f32[4,512]{1,0:T(4,128)S(1)} %add_rsqrt_fusion), kind=kLoop, calls=%fused_computation.19 | loop fusion | flops 37748736 | bytes 12597248 | tf_op jit(solution)/shard_map/convert_element_type | solution.py:33
  133.2 1.9 %collective-permute-start.2 = (bf16[4,2,1536]{2,1,0:T(2,128)(2,1)S(1)}, bf16[4,2,1536]{2,1,0:T(2,128)(2,1)S(1)}, u32[]{:S(2)}, u32[]{:S(2)}) collective-permute-start(bf16[4,2,1536]{2,1,0:T(2,128)(2,1)S(1)} %get-tuple-element.7), channel_id=1, source_target_pairs={{0,1},{1,2},{2,3},{3,4},{4,5},{5,6},{6,7},{8,9},{9,10},{10,11},{11... | collective-permute-start | bytes 73736 | tf_op jit(solution)/shard_map/ppermute | solution.py:14
  135.1 4.7 %fusion.45 = f32[4,512,384]{2,1,0:T(8,128)S(1)} fusion(bf16[4,512,1536]{2,1,0:T(8,128)(2,1)S(1)} %fusion.13, bf16[2,5,1536,384]{3,2,1,0:T(8,128)(2,1)} %param.4), kind=kOutput, calls=%fused_computation.60 | convolution fusion | flops 2415919104 | bytes 10616832 | tf_op jit(solution)/shard_map/brc,co->bro/dot_general | solution.py:24
  139.9 3.6 %collective-permute-start.3 = (bf16[4,2,1536]{2,1,0:T(2,128)(2,1)S(1)}, bf16[4,2,1536]{2,1,0:T(2,128)(2,1)S(1)}, u32[]{:S(2)}, u32[]{:S(2)}) collective-permute-start(bf16[4,2,1536]{2,1,0:T(2,128)(2,1)S(1)} %get-tuple-element.8), channel_id=1, source_target_pairs={{1,0},{2,1},{3,2},{4,3},{5,4},{6,5},{7,6},{9,8},{10,9},{11,10},{12... | collective-permute-start | bytes 73736 | tf_op jit(solution)/shard_map/ppermute | solution.py:15
  143.5 0.0 collective-permute-done.2
  143.5 4.8 %fusion.24 = f32[4,512,384]{2,1,0:T(8,128)S(1)} fusion(bf16[4,2,1536]{2,1,0:T(2,128)(2,1)S(1)} %collective-permute-done.2, bf16[4,512,1536]{2,1,0:T(8,128)(2,1)S(1)} %fusion.13, bf16[2,5,1536,384]{3,2,1,0:T(8,128)(2,1)} %param.4), kind=kOutput, calls=%fused_computation.37 | convolution fusion | flops 2428502016 | bytes 10641408 | tf_op jit(solution)/shard_map/brc,co->bro/dot_general | solution.py:24
  148.3 4.8 %fusion.34 = f32[4,512,384]{2,1,0:T(8,128)S(1)} fusion(bf16[4,512,1536]{2,1,0:T(8,128)(2,1)S(1)} %fusion.13, bf16[4,2,1536]{2,1,0:T(2,128)(2,1)S(1)} %collective-permute-done.2, bf16[2,5,1536,384]{3,2,1,0:T(8,128)(2,1)} %param.4), kind=kOutput, calls=%fused_computation.46 | convolution fusion | flops 2428502016 | bytes 10641408 | tf_op jit(solution)/shard_map/brc,co->bro/dot_general | solution.py:24
  153.2 0.0 copy-start.3
  153.2 0.0 collective-permute-done.3
  153.2 4.9 %fusion.21 = f32[4,512,384]{2,1,0:T(8,128)S(1)} fusion(bf16[4,512,1536]{2,1,0:T(8,128)(2,1)S(1)} %fusion.13, bf16[4,2,1536]{2,1,0:T(2,128)(2,1)S(1)} %collective-permute-done.3, bf16[2,5,1536,384]{3,2,1,0:T(8,128)(2,1)} %param.4), kind=kOutput, calls=%fused_computation.35 | convolution fusion | flops 2428502016 | bytes 10641408 | tf_op jit(solution)/shard_map/brc,co->bro/dot_general | solution.py:24
  158.1 0.0 copy-done.3
  158.1 5.9 %fusion.40 = bf16[1,4,512,384]{3,2,1,0:T(8,128)(2,1)S(1)} fusion(f32[4,512,384]{2,1,0:T(8,128)S(1)} %fusion.21, f32[4,512,384]{2,1,0:T(8,128)S(1)} %fusion.45, f32[4,512,384]{2,1,0:T(8,128)S(1)} %fusion.24, f32[4,512,384]{2,1,0:T(8,128)S(1)} %fusion.34, bf16[4,512,384]{2,1,0:T(8,128)(2,1)S(1)} %copy-done.3, ...), kind=kOutput, calls=%fused_computation.57 | convolution fusion | flops 2434007040 | bytes 23224320 | tf_op jit(solution)/shard_map/brc,co->bro/dot_general | solution.py:24
  164.0 2.0 %pad_maximum_fusion.8 = bf16[2,4,512,384]{3,2,1,0:T(8,128)(2,1)} fusion(bf16[1,4,512,384]{3,2,1,0:T(8,128)(2,1)S(1)} %fusion.40, bf16[1,4,512,384]{3,2,1,0:T(8,128)(2,1)S(1)} %bitcast.61), kind=kLoop, calls=%fused_computation.54 | loop fusion | flops 1572864 | bytes 6291456 | tf_op jit(solution)/shard_map/stack | solution.py:53
  (6 shorter events, 0.1 us)
Async XLA Ops:
  6.5 4.3 %copy-start.4 = (f32[2,1536]{1,0:T(2,128)S(1)}, f32[2,1536]{1,0:T(2,128)}, u32[]{:S(2)}) copy-start(f32[2,1536]{1,0:T(2,128)} %param.5) | copy-start | bytes 36868
  6.5 116.2 %all-gather.2.cloned.1.call-start = ((), (), s32[]{:S(2)}) async-start(), calls=%async_computation | async-start | bytes 7864320 | tf_op jit(solution)/shard_map/all_gather | solution.py:49
  6.5 4.6 %copy-start = (bf16[4,512,1536]{2,1,0:T(8,128)(2,1)S(1)}, bf16[4,512,1536]{2,1,0:T(8,128)(2,1)}, u32[]{:S(2)}) copy-start(bf16[4,512,1536]{2,1,0:T(8,128)(2,1)} %param.3) | copy-start | bytes 18874372
  16.9 12.0 %copy-start.2 = (bf16[4,512,1536]{2,1,0:T(8,128)(2,1)}, bf16[4,512,1536]{2,1,0:T(8,128)(2,1)S(1)}, u32[]{:S(2)}) copy-start(bf16[4,512,1536]{2,1,0:T(8,128)(2,1)S(1)} %fusion.4) | copy-start | bytes 18874372
  17.0 12.0 %collective-permute-start = (bf16[4,2,1536]{2,1,0:T(2,128)(2,1)S(1)}, bf16[4,2,1536]{2,1,0:T(2,128)(2,1)S(1)}, u32[]{:S(2)}, u32[]{:S(2)}) collective-permute-start(bf16[4,2,1536]{2,1,0:T(2,128)(2,1)S(1)} %get-tuple-element.9), channel_id=1, source_target_pairs={{0,1},{1,2},{2,3},{3,4},{4,5},{5,6},{6,7},{8,9},{9,10},{10,11},{11... | collective-permute-start | bytes 73736 | tf_op jit(solution)/shard_map/ppermute | solution.py:14
  18.9 21.1 %collective-permute-start.1 = (bf16[4,2,1536]{2,1,0:T(2,128)(2,1)S(1)}, bf16[4,2,1536]{2,1,0:T(2,128)(2,1)S(1)}, u32[]{:S(2)}, u32[]{:S(2)}) collective-permute-start(bf16[4,2,1536]{2,1,0:T(2,128)(2,1)S(1)} %get-tuple-element.10), channel_id=1, source_target_pairs={{1,0},{2,1},{3,2},{4,3},{5,4},{6,5},{7,6},{9,8},{10,9},{11,10},{12... | collective-permute-start | bytes 73736 | tf_op jit(solution)/shard_map/ppermute | solution.py:15
  29.0 6.2 %slice-start = ((s8[6291456]{0:T(1024)(128)(4,1)}), s8[2097152]{0:T(1024)(128)(4,1)S(1)}, s32[]{:S(2)}) async-start(s8[6291456]{0:T(1024)(128)(4,1)} %bitcast.59), calls=%async_computation.1 | async-start | bytes 4194304
  29.0 6.2 %slice-start.1 = ((s8[6291456]{0:T(1024)(128)(4,1)}), s8[4194304]{0:T(1024)(128)(4,1)S(1)}, s32[]{:S(2)}) async-start(s8[6291456]{0:T(1024)(128)(4,1)} %bitcast.59), calls=%async_computation.2 | async-start | bytes 8388608
  40.0 5.0 %copy-start.5 = (f32[4,512,384]{2,1,0:T(8,128)S(1)}, f32[4,512,384]{2,1,0:T(8,128)}, u32[]{:S(2)}) copy-start(f32[4,512,384]{2,1,0:T(8,128)} %fusion.53) | copy-start | bytes 9437188
  122.8 4.6 %copy-start.1 = (bf16[4,512,1536]{2,1,0:T(8,128)(2,1)S(1)}, bf16[4,512,1536]{2,1,0:T(8,128)(2,1)}, u32[]{:S(2)}) copy-start(bf16[4,512,1536]{2,1,0:T(8,128)(2,1)} %all-gather.2.cloned.1.call-done) | copy-start | bytes 18874372
  133.2 10.3 %collective-permute-start.2 = (bf16[4,2,1536]{2,1,0:T(2,128)(2,1)S(1)}, bf16[4,2,1536]{2,1,0:T(2,128)(2,1)S(1)}, u32[]{:S(2)}, u32[]{:S(2)}) collective-permute-start(bf16[4,2,1536]{2,1,0:T(2,128)(2,1)S(1)} %get-tuple-element.7), channel_id=1, source_target_pairs={{0,1},{1,2},{2,3},{3,4},{4,5},{5,6},{6,7},{8,9},{9,10},{10,11},{11... | collective-permute-start | bytes 73736 | tf_op jit(solution)/shard_map/ppermute | solution.py:14
  139.9 13.3 %collective-permute-start.3 = (bf16[4,2,1536]{2,1,0:T(2,128)(2,1)S(1)}, bf16[4,2,1536]{2,1,0:T(2,128)(2,1)S(1)}, u32[]{:S(2)}, u32[]{:S(2)}) collective-permute-start(bf16[4,2,1536]{2,1,0:T(2,128)(2,1)S(1)} %get-tuple-element.8), channel_id=1, source_target_pairs={{1,0},{2,1},{3,2},{4,3},{5,4},{6,5},{7,6},{9,8},{10,9},{11,10},{12... | collective-permute-start | bytes 73736 | tf_op jit(solution)/shard_map/ppermute | solution.py:15
  153.2 4.9 %copy-start.3 = (bf16[4,512,384]{2,1,0:T(8,128)(2,1)S(1)}, bf16[4,512,384]{2,1,0:T(8,128)(2,1)}, u32[]{:S(2)}) copy-start(bf16[4,512,384]{2,1,0:T(8,128)(2,1)} %add_convert_fusion.1) | copy-start | bytes 4718596
Sparse Core Ops, SparseCore 0:
  51.8 70.9 all-gather.1
where the time goes:
time: 174 us; the launch traced here: 173 us
  waiting for transfers between devices  71.1 us (41%)
  matrix products  54.1 us (31%)
  other arithmetic  22 us (13%)
  between operations  13.6 us (8%)
  starting transfers between devices  11.1 us (6%)
    all_gather x1, waiting for transfers between devices, local(): whole = lax.all_gather(current, 'section', axis=2, tiled=True)  71.1 us
    dot_general x10, matrix products, convolve(): jnp.einsum('brc,co->bro', padded[:, k:k + count], kernel[k], preferred_el...  54.1 us
    convert_element_type x2, other arithmetic, normed(): return jax.nn.gelu(values * scale * gain).astype(jnp.bfloat16)  11.5 us
    reduce_sum x2, other arithmetic, normed(): scale = lax.rsqrt(jnp.mean(values * values, axis=-1, keepdims=True) + 1e-06)  8.46 us
    ppermute x2, starting transfers between devices, with_halo(): after = lax.ppermute(initial, axis, down)  7.28 us
    ppermute x2, starting transfers between devices, with_halo(): before = lax.ppermute(last, axis, up)  3.84 us
  transfers between devices with their start and end apart: 5, of which 1 were waited for; matrix products, arithmetic and copies ran while one was open for 18% of the time, Pallas kernels for 0%

commit v1 on v0

--- a/solution.py
+++ b/solution.py
@@ -1,7 +1,13 @@
 import jax
 import jax.numpy as jnp
 from jax import lax
+from jax.experimental import pallas as pl
+from jax.experimental.pallas import tpu as pltpu
 from jax.sharding import PartitionSpec as P
+
+MESH = pl.DeviceIdType.MESH
+HALO = 16
+REACH = 2
 
 
 def with_halo(value, sides, width):
@@ -37,7 +43,7 @@
     return with_halo(hidden, (("seq", 1),), 2)
 
 
-def local(inputs, weights, gains):
+def plain(inputs, weights, gains):
     share = weights.shape[3]
     begin = lax.axis_index("section") * share
     hidden = normed(inputs, gains[0])
@@ -53,6 +59,311 @@
     return jnp.stack(results, axis=0)
 
 
+def gelu(v):
+    return 0.5 * v * (1.0 + jnp.tanh(0.7978845608028654 * (v + 0.044715 * (v * v * v))))
+
+
+def fused_kernel(
+    x, w, g, out, xe, hid, y, wv, acts, last, wsem, xsem, hsend, hrecv, ssem, rsem, osem
+):
+    micro, rows, chans = x.shape
+    taps, share = w.shape[1], w.shape[3]
+    span = rows + 2 * HALO
+    half = span // 2
+    part = half // 32 * 16
+    me, seq = lax.axis_index("section"), lax.axis_index("seq")
+    nseq = lax.axis_size("seq")
+
+    def ring(at):
+        r = at // 2
+        return 2 * r + (at % 2) * (1 - 2 * (r % 2)) + r % 2
+
+    place = ring(me)
+    right, left = ring((place + 1) % 4), ring((place + 3) % 4)
+    over = ring((place + 2) % 4)
+
+    for b in range(micro):
+        pltpu.make_async_copy(x.at[b], xe.at[b, pl.ds(HALO, rows)], xsem.at[b]).start()
+    for l in range(2):
+        for k in range(taps):
+            pltpu.make_async_copy(
+                w.at[l, k], wv.at[l, :, pl.ds(k * share, share)], wsem.at[l, k]
+            ).start()
+
+    barrier = pltpu.get_barrier_semaphore()
+    for to in (right, left):
+        pl.semaphore_signal(barrier, inc=1, device_id=(to, seq), device_id_type=MESH)
+
+    @pl.when(seq > 0)
+    def _():
+        pl.semaphore_signal(barrier, inc=1, device_id=(me, seq - 1), device_id_type=MESH)
+
+    @pl.when(seq < nseq - 1)
+    def _():
+        pl.semaphore_signal(barrier, inc=1, device_id=(me, seq + 1), device_id_type=MESH)
+
+    peers = 2 + jnp.where(seq > 0, 1, 0) + jnp.where(seq < nseq - 1, 1, 0)
+    pl.semaphore_wait(barrier, peers)
+
+    def halo_up():
+        return pltpu.make_async_remote_copy(
+            src_ref=x.at[:, pl.ds(rows - HALO, HALO), :],
+            dst_ref=xe.at[:, pl.ds(0, HALO), :],
+            send_sem=hsend.at[0],
+            recv_sem=hrecv.at[0],
+            device_id=(me, seq + 1),
+            device_id_type=MESH,
+        )
+
+    def halo_down():
+        return pltpu.make_async_remote_copy(
+            src_ref=x.at[:, pl.ds(0, HALO), :],
+            dst_ref=xe.at[:, pl.ds(HALO + rows, HALO), :],
+            send_sem=hsend.at[1],
+            recv_sem=hrecv.at[1],
+            device_id=(me, seq - 1),
+            device_id_type=MESH,
+        )
+
+    @pl.when(seq < nseq - 1)
+    def _():
+        halo_up().start()
+
+    @pl.when(seq > 0)
+    def _():
+        halo_down().start()
+
+    @pl.when(seq == 0)
+    def _():
+        xe[:, 0:HALO, :] = jnp.zeros((micro, HALO, chans), jnp.bfloat16)
+
+    @pl.when(seq == nseq - 1)
+    def _():
+        xe[:, HALO + rows : span, :] = jnp.zeros((micro, HALO, chans), jnp.bfloat16)
+
+    for l in range(2):
+        y[l, 0:8, :] = jnp.zeros((8, taps * share), jnp.float32)
+        y[l, span + 8 : span + 16, :] = jnp.zeros((8, taps * share), jnp.float32)
+
+    def piece(origin, b, start, size):
+        return acts.at[origin, b, pl.ds(start, size), :]
+
+    def send(origin, b, start, size, way, c, to):
+        return pltpu.make_async_remote_copy(
+            src_ref=piece(origin, b, start, size),
+            dst_ref=piece(origin, b, start, size),
+            send_sem=ssem.at[way, c],
+            recv_sem=rsem.at[way, c],
+            device_id=(to, seq),
+            device_id_type=MESH,
+        )
+
+    def direct(b, h):
+        c = 2 * b + h
+        send(me, b, h * half, half, 0, c, right).start()
+        send(me, b, h * half, half, 1, c, left).start()
+
+    def forward(b, h):
+        c = 2 * b + h
+        send(left, b, h * half, half, 0, c, left).wait_recv()
+        send(left, b, h * half, part, 2, c, right).start()
+        send(right, b, h * half, half, 1, c, right).wait_recv()
+        send(right, b, h * half + part, half - part, 3, c, left).start()
+
+    def arrived(b, h):
+        c = 2 * b + h
+        send(over, b, h * half, part, 2, c, left).wait_recv()
+        send(over, b, h * half + part, half - part, 3, c, right).wait_recv()
+
+    tile = 16
+
+    def normalize(read, l, begin, end):
+        gain = g[l : l + 1, :]
+
+        @pl.loop(0, (end - begin) // tile)
+        def _(i):
+            at = pl.multiple_of(begin + i * tile, tile)
+            v = read(at)
+            scale = lax.rsqrt(jnp.mean(v * v, axis=-1, keepdims=True) + 1e-06)
+            hid[l, pl.ds(at, tile), :] = gelu(v * scale * gain).astype(jnp.bfloat16)
+
+    def multiply(l, begin, end):
+        wide = taps * share
+        step = 512
+        for n in range(0, wide, step):
+            size = min(step, wide - n)
+            y[l, begin + 8 : end + 8, n : n + size] = jnp.dot(
+                hid[l, begin:end, :], wv[l, :, n : n + size], preferred_element_type=jnp.float32
+            )
+
+    def combine(l, begin, end, residual, store):
+        @pl.loop(0, (end - begin) // tile)
+        def _(i):
+            at = pl.multiple_of(begin + i * tile, tile)
+            total = None
+            for k in range(taps):
+                block = y[l, pl.ds(at, tile + 16), k * share : (k + 1) * share]
+                term = block[8 - REACH + k : 8 - REACH + k + tile, :]
+                total = term if total is None else total + term
+            store(at, residual(at) + total)
+
+    low = jnp.where(seq == 0, HALO, 0)
+    high = jnp.where(seq == nseq - 1, HALO + rows, span)
+    mine = pl.ds(pl.multiple_of(me * share, 128), share)
+
+    def first(b, h):
+        def read(at):
+            return xe[b, pl.ds(at, tile), :].astype(jnp.float32)
+
+        def residual(at):
+            return xe[b, pl.ds(at, tile), mine].astype(jnp.float32)
+
+        def store(at, value):
+            row = at + lax.broadcasted_iota(jnp.int32, value.shape, 0)
+            value = jnp.where((row >= low) & (row < high), value, 0.0)
+            acts[me, b, pl.ds(at, tile), :] = value.astype(jnp.bfloat16)
+
+        begin, end = ((0, half + HALO), (half + HALO, span))[h]
+        normalize(read, 0, begin, end)
+        multiply(0, begin, end)
+        combine(0, h * half, h * half + half, residual, store)
+
+    def second(b, h):
+        def read(at):
+            parts = [acts[s, b, pl.ds(at, tile), :].astype(jnp.float32) for s in range(4)]
+            return jnp.concatenate(parts, axis=-1)
+
+        def residual(at):
+            return acts[me, b, pl.ds(at, tile), :].astype(jnp.float32)
+
+        def store(at, value):
+            last[b, pl.ds(pl.multiple_of(at - HALO, tile), tile), :] = value.astype(jnp.bfloat16)
+
+        normalize(read, 1, h * half, h * half + half)
+        multiply(1, h * half, h * half + half)
+        cut = half - HALO
+        begin, end = ((HALO, cut), (cut, HALO + rows))[h]
+        combine(1, begin, end, residual, store)
+
+    def out_first(b):
+        return pltpu.make_async_copy(
+            acts.at[me, b, pl.ds(HALO, rows), :], out.at[0, b], osem.at[0, b]
+        )
+
+    def out_last(b):
+        return pltpu.make_async_copy(last.at[b], out.at[1, b], osem.at[1, b])
+
+    def weights_ready(l):
+        for k in range(taps):
+            pltpu.make_async_copy(
+                w.at[l, k], wv.at[l, :, pl.ds(k * share, share)], wsem.at[l, k]
+            ).wait()
+
+    @pl.loop(0, micro + 1)
+    def _(b):
+        @pl.when(b < micro)
+        def _():
+            pltpu.make_async_copy(x.at[b], xe.at[b, pl.ds(HALO, rows)], xsem.at[b]).wait()
+
+            @pl.when(b == 0)
+            def _():
+                @pl.when(seq > 0)
+                def _():
+                    halo_up().wait_recv()
+
+                @pl.when(seq < nseq - 1)
+                def _():
+                    halo_down().wait_recv()
+
+                weights_ready(0)
+
+            first(b, 0)
+            direct(b, 0)
+
+        @pl.when(b > 0)
+        def _():
+            forward(b - 1, 1)
+            arrived(b - 1, 0)
+
+            @pl.when(b == 1)
+            def _():
+                weights_ready(1)
+
+            second(b - 1, 0)
+
+        @pl.when(b < micro)
+        def _():
+            first(b, 1)
+            direct(b, 1)
+            out_first(b).start()
+            forward(b, 0)
+
+        @pl.when(b > 0)
+        def _():
+            arrived(b - 1, 1)
+            second(b - 1, 1)
+            out_last(b - 1).start()
+
+    @pl.when(seq < nseq - 1)
+    def _():
+        halo_up().wait_send()
+
+    @pl.when(seq > 0)
+    def _():
+        halo_down().wait_send()
+
+    @pl.loop(0, micro)
+    def _(b):
+        out_first(b).wait()
+        out_last(b).wait()
+        for h in range(2):
+            c = 2 * b + h
+            send(me, b, h * half, half, 0, c, right).wait_send()
+            send(me, b, h * half, half, 1, c, left).wait_send()
+            send(left, b, h * half, part, 2, c, right).wait_send()
+            send(right, b, h * half + part, half - part, 3, c, left).wait_send()
+
+
+def fused(inputs, weights, gains):
+    micro, rows, chans = inputs.shape
+    layers, taps, _, share = weights.shape
+    span = rows + 2 * HALO
+    chunks = 2 * micro
+    dma = pltpu.SemaphoreType.DMA
+    hbm = pl.BlockSpec(memory_space=pltpu.HBM)
+    return pl.pallas_call(
+        fused_kernel,
+        out_shape=jax.ShapeDtypeStruct((layers, micro, rows, share), jnp.bfloat16),
+        in_specs=[hbm, hbm, pl.BlockSpec(memory_space=pltpu.VMEM)],
+        out_specs=hbm,
+        scratch_shapes=[
+            pltpu.VMEM((micro, span, chans), jnp.bfloat16),
+            pltpu.VMEM((2, span, chans), jnp.bfloat16),
+            pltpu.VMEM((2, span + 16, taps * share), jnp.float32),
+            pltpu.VMEM((2, chans, taps * share), jnp.bfloat16),
+            pltpu.VMEM((4, micro, span, share), jnp.bfloat16),
+            pltpu.VMEM((micro, rows, share), jnp.bfloat16),
+            dma((2, taps)),
+            dma((micro,)),
+            dma((2,)),
+            dma((2,)),
+            dma((4, chunks)),
+            dma((4, chunks)),
+            dma((2, micro)),
+        ],
+        compiler_params=pltpu.CompilerParams(
+            collective_id=0, has_side_effects=True, vmem_limit_bytes=60 * 1024 * 1024
+        ),
+    )(inputs, weights, gains)
+
+
+def local(inputs, weights, gains):
+    square = lax.axis_size("section") == 4 and weights.shape[0] == 2
+    if square and weights.shape[3] % 128 == 0 and inputs.shape[1] % 32 == 0:
+        return fused(inputs, weights, gains)
+    return plain(inputs, weights, gains)
+
+
 def solution(mesh):
     in_specs = (P(None, "seq", None), P(None, None, None, "section"), P())
     out_specs = P(None, None, "seq", "section")

time: 174 us -> 96.2 us (0.55)
  Pallas kernels: 0 us -> 92.2 us
  waiting for transfers between devices: 71.1 us -> 0 us
  matrix products: 54.1 us -> 0 us
  other arithmetic: 22 us -> 0 us
  between operations: 13.6 us -> 0.01 us
  starting transfers between devices: 11.1 us -> 0 us
  local copies, waits for them, and re-layouts: 0.81 us -> 3.87 us
    pallas_call x0 -> x1, Pallas kernels: none -> 92.2 us  [fused(): pl.pallas_call(fused_kernel, out_shape=jax.ShapeDtypeStruct((layers, micr...]
    all_gather x1 -> x0, waiting for transfers between devices: 71.1 us -> none  [local(): whole = lax.all_gather(current, 'section', axis=2, tiled=True)]
    dot_general x10 -> x0, matrix products: 54.1 us -> none  [convolve(): jnp.einsum('brc,co->bro', padded[:, k:k + count], kernel[k], preferred_el...]
    convert_element_type x2 -> x0, other arithmetic: 11.5 us -> none  [normed(): return jax.nn.gelu(values * scale * gain).astype(jnp.bfloat16)]
    ppermute x4 -> x0, starting transfers between devices: 11.1 us -> none  [the longest x2 7.28 us: with_halo(): after = lax.ppermute(initial, axis, down)]
    reduce_sum x2 -> x0, other arithmetic: 8.46 us -> none  [normed(): scale = lax.rsqrt(jnp.mean(values * values, axis=-1, keepdims=True) + 1e-06)]
    unnamed x16 -> x1, local copies, waits for them, and re-layouts: 0.69 us -> 3.87 us
    another operation x1 -> x0, other arithmetic: 2.02 us -> none  [local(): return jnp.stack(results, axis=0)]
  transfers between devices with their start and end apart: 5 -> 0, of which waited for: 1 -> 0; matrix products, arithmetic and copies ran while one was open for 18% -> 0% of each run, Pallas kernels for 0% -> 0%
where the time goes in v1:
time: 96.2 us; the launch traced here: 96 us
  Pallas kernels  92.2 us (96%)
  local copies, waits for them, and re-layouts  3.87 us (4%)
    pallas_call x1, Pallas kernels, fused(): pl.pallas_call(fused_kernel, out_shape=jax.ShapeDtypeStruct((layers, micr...  92.2 us
    unnamed x1, local copies, waits for them, and re-layouts  3.87 us

profile of v1, /device:TPU:16, one launch (start us, length us, event | category | flops | bytes accessed | tf_op | source)
XLA Modules:
  0.0 96.0 jit_solution(10412947485383565488)
XLA Ops:
  0.0 92.2 %shard_map.37 = bf16[2,4,512,384]{3,2,1,0:T(8,128)(2,1)} custom-call(bf16[4,512,1536]{2,1,0:T(8,128)(2,1)} %x.1, bf16[2,5,1536,384]{3,2,1,0:T(8,128)(2,1)} %w.1, f32[2,1536]{1,0:T(2,128)} %g.1), custom_call_target="tpu_custom_call" | custom-call | tf_op jit(solution)/shard_map/pallas_call | solution.py:334
  92.2 3.9 %copy.5 = bf16[2,4,512,384]{3,2,1,0:T(8,128)(2,1)} copy(bf16[2,4,512,384]{3,2,1,0:T(8,128)(2,1)} %shard_map.37) | data formatting | bytes 6291456
